TPU v7x, 32 devices: a whole 2x2x4 slice. The times are simulated.
32 devices in a mesh: feed: 8 (over z, x), tm: 4 (over y, core).
Axes of the slice: x: 2, y: 2, z: 4, core: 2. Of those that a mesh axis runs over, the one named last changes fastest.
Arguments:
- voltages: bfloat16 [2048, 131072], P('feed', 'tm'), may hold values from -6 to 6
- feed_slot: int32 [2048], replicated, may hold values from 0 to 2047, each once
- channel_flags: int32 [1024], replicated, may hold values from 0 to 1, as said below
Outputs:
- beam_power: float32 [96, 16, 1024], P(('feed', 'tm'))
Inputs may be any that keep to these rules, and one draw needn't show every extreme that they name: `channel_flags`: exactly 96 entries are 1. `feed_slot`: each slot is named by exactly one input.
All inputs are finite; a program needn't handle non-finite values.
Results may differ from a plain program's by a relative error of at most 0.01.
Values may be sent and summed in bfloat16 or wider, within the bound.
A program may use at most 128 MiB of HBM per device.

v0:
```python
import math

import functools

import jax
import jax.numpy as jnp
import numpy as np
from jax import lax
from jax.experimental import pallas as pl
from jax.experimental.pallas import tpu as pltpu
from jax.sharding import PartitionSpec as P

CHANNELS = 1024
TAPS = 4
CYL = 4
NS = 256
UPCH = 16
LIVE_DEV = 3


def passed_along(block, axis, distance):
    devices = range(lax.axis_size(axis))
    route = [(i - distance, i) for i in devices if i - distance in devices]
    return lax.ppermute(block, axis, route)


def pfb_window():
    length = TAPS * 2 * CHANNELS
    sample = jnp.arange(length, dtype=jnp.float32)
    offset = (sample - length / 2 + 0.5) / (2 * CHANNELS)
    taper = 0.5 - 0.5 * jnp.cos(2.0 * jnp.pi * (sample + 0.5) / length)
    return (jnp.sinc(offset) * taper).reshape(TAPS, 2 * CHANNELS)


def phase_pair(modulus, first, second, scale):
    product = first[:, None] * second[None, :] % modulus
    angle = product.astype(jnp.float32) * (2.0 * jnp.pi / modulus)
    return (jnp.cos(angle) * scale, jnp.sin(angle) * scale)


def grid_table():
    index = jnp.arange(NS, dtype=jnp.int32)
    cosine, sine = phase_pair(NS, index, index, 1.0 / math.sqrt(NS))
    cosine = cosine.astype(jnp.bfloat16)
    sine = sine.astype(jnp.bfloat16)
    return cosine, sine


def live_channels(flags, count):
    k = jnp.arange(flags.shape[0], dtype=jnp.int32)
    seen = jnp.sum(jnp.where(k[None, :] <= k[:, None], flags[None, :], 0), axis=1)
    j = jnp.arange(count, dtype=jnp.int32)
    return jnp.sum((seen[None, :] <= j[:, None]).astype(jnp.int32), axis=1)


def pfb_filter(voltages, n_frames, window):
    inputs = voltages.shape[0]
    frames = voltages.reshape(inputs, n_frames, 2 * CHANNELS).astype(jnp.float32)
    padded = jnp.pad(frames, ((0, 0), (TAPS - 1, TAPS - 1), (0, 0)))
    total = n_frames + TAPS - 1
    summed = 0.0
    for tap in range(TAPS):
        summed = summed + window[tap] * padded[:, tap : tap + total]
    return summed.astype(jnp.bfloat16)


def local_plain(voltages, feed_slot, channel_flags):
    n_frames = voltages.shape[1] // (2 * CHANNELS)
    n_time = lax.axis_size("tm")
    n_feed = lax.axis_size("feed")
    inputs = voltages.shape[0]
    live_count = LIVE_DEV * n_feed * n_time
    chans = LIVE_DEV * n_time
    live = live_channels(channel_flags, live_count)
    cosine, sine = phase_pair(
        2 * CHANNELS, live, jnp.arange(2 * CHANNELS, dtype=jnp.int32), 1.0 / math.sqrt(2 * CHANNELS)
    )
    coeffs = jnp.stack([cosine, -sine]).astype(jnp.bfloat16)
    filtered = pfb_filter(voltages, n_frames, pfb_window())
    spectra = jnp.einsum("rcs,ifs->rcfi", coeffs, filtered, preferred_element_type=jnp.float32)
    earlier = passed_along(spectra[:, :, n_frames:].astype(jnp.bfloat16), "tm", 1)
    spectra = spectra[:, :, :n_frames]
    spectra = jnp.concatenate(
        [spectra[:, :, : TAPS - 1] + earlier.astype(jnp.float32), spectra[:, :, TAPS - 1 :]], axis=2
    ).astype(jnp.bfloat16)
    turned = lax.all_to_all(
        spectra.reshape(2, n_feed, chans, n_frames, inputs), "feed", split_axis=1, concat_axis=1, tiled=True
    )
    slots = feed_slot.reshape(n_feed, inputs)
    onehot = (slots[:, :, None] == jnp.arange(n_feed * inputs, dtype=jnp.int32)).astype(jnp.bfloat16)
    cells = jnp.einsum(
        "rscfi,sin->rcfn", turned, onehot, preferred_element_type=jnp.float32
    ).astype(jnp.bfloat16)
    cells = cells.reshape(2, chans, n_frames, 2 * CYL, NS)
    cosine, sine = grid_table()
    table = jnp.stack([jnp.stack([cosine, -sine], axis=1), jnp.stack([sine, cosine], axis=1)])
    ns_out = jnp.einsum("rcfgm,rmqn->qcfgn", cells, table, preferred_element_type=jnp.float32)
    z = ns_out.reshape(2, chans, n_frames, 2, CYL, NS)
    re, im = z[0], z[1]
    r = [re[:, :, :, y] for y in range(CYL)]
    i = [im[:, :, :, y] for y in range(CYL)]
    t0r, t1r, t2r, t3r = r[0] + r[2], r[0] - r[2], r[1] + r[3], r[1] - r[3]
    t0i, t1i, t2i, t3i = i[0] + i[2], i[0] - i[2], i[1] + i[3], i[1] - i[3]
    beam_re = jnp.stack([t0r + t2r, t1r + t3i, t0r - t2r, t1r - t3i], axis=3)
    beam_im = jnp.stack([t0i + t2i, t1i - t3r, t0i - t2i, t1i + t3r], axis=3)
    beams = (jnp.stack([beam_re, beam_im]) * 0.5).astype(jnp.bfloat16)
    blocks = n_frames // UPCH
    beams = beams.reshape(2, chans, blocks, UPCH, 2, CYL * NS)
    index = jnp.arange(UPCH, dtype=jnp.int32)
    up_cos, up_sin = phase_pair(UPCH, index, index, 1.0 / math.sqrt(UPCH))
    up_cos = up_cos.astype(jnp.bfloat16)
    up_sin = up_sin.astype(jnp.bfloat16)
    up_table = jnp.stack([jnp.stack([up_cos, -up_sin], axis=1), jnp.stack([up_sin, up_cos], axis=1)])
    up = jnp.einsum("qcbupn,quvk->vcbkpn", beams, up_table, preferred_element_type=jnp.float32)
    power = jnp.sum(up * up, axis=(0, 2, 4)) * (1.0 / (2.0 * n_time * blocks))
    parts = lax.all_to_all(
        power.astype(jnp.bfloat16).reshape(n_time, LIVE_DEV, UPCH, CYL * NS), "tm", split_axis=0, concat_axis=0, tiled=True
    )
    return jnp.sum(parts.astype(jnp.float32), axis=0)


MESH = pl.DeviceIdType.MESH
NT = (((1,), (1,)), ((), ()))


def fused_kernel(
    n_feed, n_time, n_frames, scale,
    volt, trig, window, slots, t1, t2, upm, out,
    vp, coeffs, filt, tmp, send, recv, hist_out, hist_in, onehot, acc, beams, power, psend, precv,
    load_sem, own_sem, hist_sem, send_sem, recv_sem, psend_sem, precv_sem,
):
    me = lax.axis_index("feed")
    tm = lax.axis_index("tm")
    frame = 2 * CHANNELS
    past = TAPS - 1
    quads = n_frames // 4
    inputs = volt.shape[0]
    rows = coeffs.shape[0]
    own_rows = LIVE_DEV * UPCH

    def partner(m):
        far = lax.rem(me // 4 + m // 4, 2)
        near = lax.rem(lax.rem(me // 2, 2) + lax.rem(m // 2, 2), 2)
        return far * 4 + near * 2 + lax.rem(lax.rem(me, 2) + lax.rem(m, 2), 2)

    def load(f):
        return pltpu.make_async_copy(
            volt.at[:, f * frame : (f + 1) * frame], vp.at[f + past], load_sem.at[f]
        )

    order = list(range(1, n_frames)) + [0]
    for f in order:
        load(f).start()
    barrier = pltpu.get_barrier_semaphore()
    for o in range(1, n_feed):
        pl.semaphore_signal(barrier, inc=1, device_id={"feed": lax.rem(me + o, n_feed)}, device_id_type=MESH)
    for o in range(1, n_time):
        pl.semaphore_signal(barrier, inc=1, device_id={"tm": lax.rem(tm + o, n_time)}, device_id_type=MESH)

    for k in range(frame // 128):
        value = trig[:, 256 + k : 257 + k] * trig[:, :128]
        value = value - trig[:, 256 + frame // 128 + k : 257 + frame // 128 + k] * trig[:, 128:256]
        coeffs[:, k * 128 : (k + 1) * 128] = (value * (1.0 / math.sqrt(frame))).astype(jnp.bfloat16)

    def spectra(f):
        width = 256

        def chunk(c, _):
            lanes = pl.ds(pl.multiple_of(c * width, width), width)
            total = window[0:1, lanes] * vp[f, :, lanes].astype(jnp.float32)
            for t in range(1, TAPS):
                total = total + window[t : t + 1, lanes] * vp[f + t, :, lanes].astype(jnp.float32)
            filt[:, lanes] = total.astype(jnp.bfloat16)
            return 0

        lax.fori_loop(0, frame // width, chunk, 0)
        return lax.dot_general(coeffs[...], filt[...], NT, preferred_element_type=jnp.float32)

    def hist_copy(to):
        return pltpu.make_async_remote_copy(
            src_ref=hist_out, dst_ref=hist_in, send_sem=hist_sem.at[0], recv_sem=hist_sem.at[1],
            device_id={"tm": to}, device_id_type=MESH,
        )

    def send_copy(q, m):
        to = partner(m)
        return pltpu.make_async_remote_copy(
            src_ref=send.at[q, to], dst_ref=recv.at[me, q],
            send_sem=send_sem.at[q, m], recv_sem=recv_sem.at[q, m],
            device_id={"feed": to}, device_id_type=MESH,
        )

    def arrival(q, m):
        back = partner(m)
        return pltpu.make_async_remote_copy(
            src_ref=send.at[q, back], dst_ref=recv.at[back, q],
            send_sem=send_sem.at[q, m], recv_sem=recv_sem.at[q, m],
            device_id={"feed": back}, device_id_type=MESH,
        )

    def own_copy(q):
        return pltpu.make_async_copy(send.at[q, me], recv.at[me, q], own_sem.at[q])

    def far_first(k):
        return lax.rem(k + n_feed // 2 - 1, n_feed - 1) + 1

    lower = lax.broadcasted_iota(jnp.int32, (8, inputs), 0) < 4

    def quad(q, first):
        def one(k, _):
            value = spectra(q * 4 + k)
            if first:
                value = value + jnp.where(k < past, 1.0, 0.0) * hist_in[jnp.minimum(k, past - 1)].astype(jnp.float32)
            tmp[k] = value
            return 0

        lax.fori_loop(0, 4, one, 0)

        def pack(d, _):
            parts = [[], []]
            at = pl.multiple_of(d * 24, 8)
            for pair in range(2):
                a0, b0, c0 = (tmp[2 * pair, pl.ds(at + 8 * k, 8)] for k in range(3))
                a1, b1, c1 = (tmp[2 * pair + 1, pl.ds(at + 8 * k, 8)] for k in range(3))
                parts[0] += [a0, a1, jnp.where(lower, b0, pltpu.roll(b1, 4, 0))]
                parts[1] += [c0, c1, jnp.where(lower, pltpu.roll(b0, 4, 0), b1)]
            send[q, d, 0] = jnp.concatenate(parts[0], axis=0).astype(jnp.bfloat16)
            send[q, d, 1] = jnp.concatenate(parts[1], axis=0).astype(jnp.bfloat16)
            return 0

        lax.fori_loop(0, n_feed, pack, 0)

        if q == 1:
            pl.semaphore_wait(barrier, n_feed - 1 + n_time - 1)

        def start(k, _):
            send_copy(q, far_first(k)).start()
            return 0

        lax.fori_loop(0, n_feed - 1, start, 0)
        own_copy(q).start()

    def tail_frames():
        def tail_frame(k, _):
            hist_out[k] = spectra(n_frames + k).astype(jnp.bfloat16)
            return 0

        lax.fori_loop(0, past, tail_frame, 0)

        @pl.when(tm < n_time - 1)
        def _():
            hist_copy(lax.rem(tm + 1, n_time)).start()

    for f in range(1, 8):
        load(f).wait()
    quad(1, False)
    for t in range(past):
        vp[t] = jnp.zeros_like(vp[t])
        vp[n_frames + past + t] = jnp.zeros_like(vp[t])
    for q in range(2, quads):
        for f in range(4 * q, 4 * q + 4):
            load(f).wait()
        if q == quads - 1:
            tail_frames()
        quad(q, False)
    load(0).wait()

    @pl.when(tm > 0)
    def _():
        hist_copy(lax.rem(tm + n_time - 1, n_time)).wait_recv()

    @pl.when(tm == 0)
    def _():
        hist_in[...] = jnp.zeros_like(hist_in)

    quad(0, True)

    total = n_feed * inputs
    which = lax.broadcasted_iota(jnp.int32, (total, inputs), 0)

    def ones(s, _):
        onehot[s] = jnp.where(which == slots[s], 1.0, 0.0).astype(jnp.bfloat16)
        return 0

    lax.fori_loop(0, n_feed, ones, 0)

    step = 512

    def place(s, lo, hi, fresh):
        count = hi - lo
        block = recv[s, lo:hi].reshape(count * 96, inputs)

        def part(n, _):
            at = pl.multiple_of(n * step, step)
            got = lax.dot_general(block, onehot[s, pl.ds(at, step), :], NT, preferred_element_type=jnp.float32)
            got = got.reshape(count, 2, 48, step)
            if fresh:
                acc[lo:hi, :, :, pl.ds(at, step)] = got
            else:
                acc[lo:hi, :, :, pl.ds(at, step)] += got
            return 0

        lax.fori_loop(0, total // step, part, 0)

    def gather(lo, hi):
        for q in range(lo, hi):
            own_copy(q).wait()
        place(me, lo, hi, True)

        def source(k, _):
            for q in range(lo, hi):
                arrival(q, k + 1).wait_recv()
            place(partner(k + 1), lo, hi, False)
            return 0

        lax.fori_loop(0, n_feed - 1, source, 0)

    def beamform(lo, hi):
        count = hi - lo

        def cells(part, at):
            return acc[lo:hi, part, :, at : at + NS].reshape(count * 48, NS).astype(jnp.bfloat16)

        stacked = [jnp.concatenate([cells(part, g * NS) for g in range(2 * CYL)], axis=0) for part in range(2)]
        value = jnp.dot(stacked[0], t1[...], preferred_element_type=jnp.float32)
        value = value + jnp.dot(stacked[1], t2[...], preferred_element_type=jnp.float32)
        for p in range(2):
            z = []
            for y in range(CYL):
                one = value[(p * CYL + y) * count * 48 : (p * CYL + y + 1) * count * 48]
                z.append((one[:, :NS], one[:, NS:]))
            (r0, i0), (r1, i1), (r2, i2), (r3, i3) = z
            t0r, t1r, t2r, t3r = r0 + r2, r0 - r2, r1 + r3, r1 - r3
            t0i, t1i, t2i, t3i = i0 + i2, i0 - i2, i1 + i3, i1 - i3
            re = [t0r + t2r, t1r + t3i, t0r - t2r, t1r - t3i]
            im = [t0i + t2i, t1i - t3r, t0i - t2i, t1i + t3r]
            for e in range(CYL):
                at = (p * CYL + e) * NS
                for part, beam in ((0, re[e]), (1, im[e])):
                    beams[part, lo:hi, :, at : at + NS] = (beam * 0.5).astype(jnp.bfloat16).reshape(count, 48, NS)

    gather(1, quads)
    beamform(1, quads)
    gather(0, 1)
    beamform(0, 1)

    def power_copy(o, e):
        to = lax.rem(tm + o, n_time)
        return pltpu.make_async_remote_copy(
            src_ref=psend.at[e, to], dst_ref=precv.at[o - 1, e],
            send_sem=psend_sem.at[o - 1, e], recv_sem=precv_sem.at[o - 1, e],
            device_id={"tm": to}, device_id_type=MESH,
        )

    outs = upm.shape[0] // 2
    for e in range(CYL):
        summed = 0.0
        for p in range(2):
            at = (p * CYL + e) * NS
            up = jnp.dot(upm[...], beams[:, :, :, at : at + NS].reshape(-1, NS), preferred_element_type=jnp.float32)
            summed = summed + up[:outs] * up[:outs] + up[outs:] * up[outs:]
        summed = (summed * scale).reshape(n_time, own_rows, NS)
        power[e] = summed
        psend[e] = summed.astype(jnp.bfloat16)
        for o in range(1, n_time):
            power_copy(o, e).start()
    for e in range(CYL):
        result = power[e, tm]
        for o in range(1, n_time):
            power_copy(o, e).wait_recv()
            result = result + precv[o - 1, e].astype(jnp.float32)
        out[:, e * NS : (e + 1) * NS] = result
    for e in range(CYL):
        for o in range(1, n_time):
            power_copy(o, e).wait_send()

    def drain(k, _):
        for q in range(quads):
            send_copy(q, k + 1).wait_send()
        return 0

    lax.fori_loop(0, n_feed - 1, drain, 0)

    @pl.when(tm < n_time - 1)
    def _():
        hist_copy(lax.rem(tm + 1, n_time)).wait_send()


def row_order(quads):
    frames, chans = [], []
    for q in range(quads):
        for pair in range(2):
            f = 4 * q + 2 * pair
            frames += [f] * 8 + [f + 1] * 8 + [f] * 4 + [f + 1] * 4
            chans += list(range(8)) * 2 + list(range(8, 12)) * 2
    return np.array(frames), np.array(chans)


def rounded_pair(modulus, first, second):
    angle = (first[:, None] * second[None, :] % modulus) * (2.0 * np.pi / modulus)
    scale = 1.0 / np.sqrt(modulus)
    bf16 = jnp.bfloat16
    return (
        (np.cos(angle) * scale).astype(np.float32).astype(bf16),
        (np.sin(angle) * scale).astype(np.float32).astype(bf16),
    )


def window_table():
    length = TAPS * 2 * CHANNELS
    sample = np.arange(length)
    offset = (sample - length / 2 + 0.5) / (2 * CHANNELS)
    taper = 0.5 - 0.5 * np.cos(2.0 * np.pi * (sample + 0.5) / length)
    return (np.sinc(offset) * taper).astype(np.float32).reshape(TAPS, 2 * CHANNELS)


def local_fused(voltages, feed_slot, channel_flags):
    bf16 = jnp.bfloat16
    frame = 2 * CHANNELS
    inputs = voltages.shape[0]
    n_frames = voltages.shape[1] // frame
    n_time = lax.axis_size("tm")
    n_feed = lax.axis_size("feed")
    chans = LIVE_DEV * n_time
    quads = n_frames // 4
    live = live_channels(channel_flags, chans * n_feed).reshape(n_feed, chans)
    row_chan = jnp.concatenate([live, live[:, 8:], live[:, :8]], axis=1).reshape(-1)
    quarter = frame // 4
    shift = np.tile(np.where(np.arange(2 * chans) >= chans, quarter, 0), n_feed)
    fine = np.arange(128)
    coarse = np.arange(frame // 128) * 128
    step = jnp.array(np.concatenate([fine, fine, coarse, coarse]), jnp.int32)
    lag = np.concatenate([fine * 0, fine * 0 + quarter, coarse * 0, coarse * 0 + quarter])
    turned = np.concatenate([fine * 0, fine * 0, coarse * 0 + 1, coarse * 0 + 1])
    extra = jnp.array(shift[:, None] * turned[None, :] + frame - lag[None, :], jnp.int32)
    product = (row_chan[:, None] * step[None, :] + extra) & (frame - 1)
    trig = jnp.cos(product.astype(jnp.float32) * (2.0 * jnp.pi / frame))
    index = np.arange(NS)
    c, d = rounded_pair(NS, index, index)
    t1 = jnp.array(np.concatenate([c, -d], axis=1))
    t2 = jnp.array(np.concatenate([d, c], axis=1))
    frames, row_ch = row_order(quads)
    up_cos, up_sin = rounded_pair(UPCH, np.arange(UPCH), frames)
    same = (np.arange(chans)[:, None] == row_ch[None, :])[:, None, :].astype(np.float32)
    cm = (same * up_cos.astype(np.float32)[None]).reshape(chans * UPCH, -1)
    sm = (same * up_sin.astype(np.float32)[None]).reshape(chans * UPCH, -1)
    upm = np.concatenate([np.concatenate([cm, sm], 1), np.concatenate([-sm, cm], 1)], 0)
    upm = jnp.array(upm.astype(bf16))
    rows = 2 * chans * n_feed
    total = n_feed * inputs
    own_rows = LIVE_DEV * UPCH
    vmem = pl.BlockSpec(memory_space=pltpu.VMEM)
    dma = pltpu.SemaphoreType.DMA
    result = pl.pallas_call(
        functools.partial(fused_kernel, n_feed, n_time, n_frames, 1.0 / (2.0 * n_time)),
        out_shape=jax.ShapeDtypeStruct((own_rows, CYL * NS), jnp.float32),
        in_specs=[pl.BlockSpec(memory_space=pl.ANY)] + [vmem] * 6,
        out_specs=vmem,
        scratch_shapes=[
            pltpu.VMEM((n_frames + 2 * TAPS - 2, inputs, frame), bf16),
            pltpu.VMEM((rows, frame), bf16),
            pltpu.VMEM((inputs, frame), bf16),
            pltpu.VMEM((4, rows, inputs), jnp.float32),
            pltpu.VMEM((quads, n_feed, 2, 48, inputs), bf16),
            pltpu.VMEM((n_feed, quads, 2, 48, inputs), bf16),
            pltpu.VMEM((TAPS - 1, rows, inputs), bf16),
            pltpu.VMEM((TAPS - 1, rows, inputs), bf16),
            pltpu.VMEM((n_feed, total, inputs), bf16),
            pltpu.VMEM((quads, 2, 48, total), jnp.float32),
            pltpu.VMEM((2, quads, 48, total), bf16),
            pltpu.VMEM((CYL, n_time, own_rows, NS), jnp.float32),
            pltpu.VMEM((CYL, n_time, own_rows, NS), bf16),
            pltpu.VMEM((n_time - 1, CYL, own_rows, NS), bf16),
            dma((n_frames,)),
            dma((quads,)),
            dma((2,)),
            dma((quads, n_feed)),
            dma((quads, n_feed)),
            dma((n_time - 1, CYL)),
            dma((n_time - 1, CYL)),
        ],
        compiler_params=pltpu.CompilerParams(
            collective_id=0, has_side_effects=True, vmem_limit_bytes=62 * 1024 * 1024
        ),
    )(voltages, trig, jnp.array(window_table()), feed_slot.reshape(n_feed, 1, inputs), t1, t2, upm)
    return result.reshape(LIVE_DEV, UPCH, CYL * NS)


def local(voltages, feed_slot, channel_flags):
    fits = (
        voltages.shape[0] == NS
        and voltages.shape[1] == UPCH * 2 * CHANNELS
        and lax.axis_size("tm") == 4
        and lax.axis_size("feed") == 8
        and lax.axis_size("feed") * voltages.shape[0] == 2 * CYL * NS
    )
    return (local_fused if fits else local_plain)(voltages, feed_slot, channel_flags)


def solution(mesh):
    in_specs = (P("feed", "tm"), P(), P())
    out_specs = P(("feed", "tm"), None, None)
    return jax.shard_map(local, mesh=mesh, in_specs=in_specs, out_specs=out_specs, check_vma=False)
```

profile of v0, /device:TPU:0, one launch (start us, length us, event | category | flops | bytes accessed | tf_op | source)
XLA Modules:
  0.0 68.4 jit_solution(12433542785398397555)
XLA Ops:
  0.0 0.9 %select_reduce_fusion = s32[1024]{0:T(1024)S(1)} fusion(s32[1024]{0:T(1024)} %param.11), kind=kLoop, calls=%fused_computation | loop fusion | flops 3144704 | bytes 8192 | tf_op jit(solution)/shard_map/reduce_sum | solution.py:51
  0.9 0.1 convert_reduce_fusion
  1.0 0.1 reshape.13
  1.1 0.1 slice.6
  1.2 0.1 pad_add_fusion
  1.3 0.1 mul.21
  1.3 2.7 %multiply_cosine_fusion.trig = f32[192,288]{1,0:T(8,128)} fusion(s32[192,288]{1,0:T(8,128)} %constant.19.clone, s32[288]{0:T(512)} %constant.18.clone, s32[192]{0:T(256)S(1)} %mul.21), kind=kLoop, calls=%fused_computation.4 | loop fusion | flops 276480 | bytes 444288 | tf_op jit(solution)/shard_map/cos | solution.py:437
  4.1 62.6 %shard_map.91 = f32[48,1024]{1,0:T(8,128)} custom-call(bf16[256,32768]{1,0:T(8,128)(2,1)} %volt.1, f32[192,288]{1,0:T(8,128)} %multiply_cosine_fusion.trig, f32[4,2048]{1,0:T(4,128)} %constant.23.clone.window, s32[8,1,256]{2,1,0:T(1,128)} %bitcast.5, bf16[256,512]{1,0:T(8,128)(2,1)} %constant.20.clone.t1, bf16[256,512]{1,0:T(8,128)(2,1)} %constant.21.clone.t2, ...), custom_call_target="tpu_custom_call" | custom-call | tf_op jit(solution)/shard_map/pallas_call | solution.py:454
  66.7 1.6 %copy.11 = f32[3,16,1024]{2,1,0:T(8,128)} copy(f32[3,16,1024]{2,1,0:T(8,128)} %bitcast.3) | data formatting | bytes 393216
where the time goes:
time: 68.6 us; the launch traced here: 68.4 us
  Pallas kernels  62.6 us (91%)
  other arithmetic  3.85 us (6%)
  local copies, waits for them, and re-layouts  1.85 us (3%)
    pallas_call x1, Pallas kernels, local_fused(): pl.pallas_call(functools.partial(fused_kernel, n_feed, n_time, n_frames,...  62.6 us
    cos x1, other arithmetic, local_fused(): trig = jnp.cos(product.astype(jnp.float32) * (2.0 * jnp.pi / frame))  2.75 us
    unnamed x1, local copies, waits for them, and re-layouts  1.62 us

commit v1 on v0

v1 whole, which is shorter than its diff:
```python
import math

import functools

import jax
import jax.numpy as jnp
import numpy as np
from jax import lax
from jax.experimental import pallas as pl
from jax.experimental.pallas import tpu as pltpu
from jax.sharding import PartitionSpec as P

CHANNELS = 1024
TAPS = 4
CYL = 4
NS = 256
UPCH = 16
LIVE_DEV = 3


def passed_along(block, axis, distance):
    devices = range(lax.axis_size(axis))
    route = [(i - distance, i) for i in devices if i - distance in devices]
    return lax.ppermute(block, axis, route)


def pfb_window():
    length = TAPS * 2 * CHANNELS
    sample = jnp.arange(length, dtype=jnp.float32)
    offset = (sample - length / 2 + 0.5) / (2 * CHANNELS)
    taper = 0.5 - 0.5 * jnp.cos(2.0 * jnp.pi * (sample + 0.5) / length)
    return (jnp.sinc(offset) * taper).reshape(TAPS, 2 * CHANNELS)


def phase_pair(modulus, first, second, scale):
    product = first[:, None] * second[None, :] % modulus
    angle = product.astype(jnp.float32) * (2.0 * jnp.pi / modulus)
    return (jnp.cos(angle) * scale, jnp.sin(angle) * scale)


def grid_table():
    index = jnp.arange(NS, dtype=jnp.int32)
    cosine, sine = phase_pair(NS, index, index, 1.0 / math.sqrt(NS))
    cosine = cosine.astype(jnp.bfloat16)
    sine = sine.astype(jnp.bfloat16)
    return cosine, sine


def live_channels(flags, count):
    k = jnp.arange(flags.shape[0], dtype=jnp.int32)
    seen = jnp.sum(jnp.where(k[None, :] <= k[:, None], flags[None, :], 0), axis=1)
    j = jnp.arange(count, dtype=jnp.int32)
    return jnp.sum((seen[None, :] <= j[:, None]).astype(jnp.int32), axis=1)


def pfb_filter(voltages, n_frames, window):
    inputs = voltages.shape[0]
    frames = voltages.reshape(inputs, n_frames, 2 * CHANNELS).astype(jnp.float32)
    padded = jnp.pad(frames, ((0, 0), (TAPS - 1, TAPS - 1), (0, 0)))
    total = n_frames + TAPS - 1
    summed = 0.0
    for tap in range(TAPS):
        summed = summed + window[tap] * padded[:, tap : tap + total]
    return summed.astype(jnp.bfloat16)


def local_plain(voltages, feed_slot, channel_flags):
    n_frames = voltages.shape[1] // (2 * CHANNELS)
    n_time = lax.axis_size("tm")
    n_feed = lax.axis_size("feed")
    inputs = voltages.shape[0]
    live_count = LIVE_DEV * n_feed * n_time
    chans = LIVE_DEV * n_time
    live = live_channels(channel_flags, live_count)
    cosine, sine = phase_pair(
        2 * CHANNELS, live, jnp.arange(2 * CHANNELS, dtype=jnp.int32), 1.0 / math.sqrt(2 * CHANNELS)
    )
    coeffs = jnp.stack([cosine, -sine]).astype(jnp.bfloat16)
    filtered = pfb_filter(voltages, n_frames, pfb_window())
    spectra = jnp.einsum("rcs,ifs->rcfi", coeffs, filtered, preferred_element_type=jnp.float32)
    earlier = passed_along(spectra[:, :, n_frames:].astype(jnp.bfloat16), "tm", 1)
    spectra = spectra[:, :, :n_frames]
    spectra = jnp.concatenate(
        [spectra[:, :, : TAPS - 1] + earlier.astype(jnp.float32), spectra[:, :, TAPS - 1 :]], axis=2
    ).astype(jnp.bfloat16)
    turned = lax.all_to_all(
        spectra.reshape(2, n_feed, chans, n_frames, inputs), "feed", split_axis=1, concat_axis=1, tiled=True
    )
    slots = feed_slot.reshape(n_feed, inputs)
    onehot = (slots[:, :, None] == jnp.arange(n_feed * inputs, dtype=jnp.int32)).astype(jnp.bfloat16)
    cells = jnp.einsum(
        "rscfi,sin->rcfn", turned, onehot, preferred_element_type=jnp.float32
    ).astype(jnp.bfloat16)
    cells = cells.reshape(2, chans, n_frames, 2 * CYL, NS)
    cosine, sine = grid_table()
    table = jnp.stack([jnp.stack([cosine, -sine], axis=1), jnp.stack([sine, cosine], axis=1)])
    ns_out = jnp.einsum("rcfgm,rmqn->qcfgn", cells, table, preferred_element_type=jnp.float32)
    z = ns_out.reshape(2, chans, n_frames, 2, CYL, NS)
    re, im = z[0], z[1]
    r = [re[:, :, :, y] for y in range(CYL)]
    i = [im[:, :, :, y] for y in range(CYL)]
    t0r, t1r, t2r, t3r = r[0] + r[2], r[0] - r[2], r[1] + r[3], r[1] - r[3]
    t0i, t1i, t2i, t3i = i[0] + i[2], i[0] - i[2], i[1] + i[3], i[1] - i[3]
    beam_re = jnp.stack([t0r + t2r, t1r + t3i, t0r - t2r, t1r - t3i], axis=3)
    beam_im = jnp.stack([t0i + t2i, t1i - t3r, t0i - t2i, t1i + t3r], axis=3)
    beams = (jnp.stack([beam_re, beam_im]) * 0.5).astype(jnp.bfloat16)
    blocks = n_frames // UPCH
    beams = beams.reshape(2, chans, blocks, UPCH, 2, CYL * NS)
    index = jnp.arange(UPCH, dtype=jnp.int32)
    up_cos, up_sin = phase_pair(UPCH, index, index, 1.0 / math.sqrt(UPCH))
    up_cos = up_cos.astype(jnp.bfloat16)
    up_sin = up_sin.astype(jnp.bfloat16)
    up_table = jnp.stack([jnp.stack([up_cos, -up_sin], axis=1), jnp.stack([up_sin, up_cos], axis=1)])
    up = jnp.einsum("qcbupn,quvk->vcbkpn", beams, up_table, preferred_element_type=jnp.float32)
    power = jnp.sum(up * up, axis=(0, 2, 4)) * (1.0 / (2.0 * n_time * blocks))
    parts = lax.all_to_all(
        power.astype(jnp.bfloat16).reshape(n_time, LIVE_DEV, UPCH, CYL * NS), "tm", split_axis=0, concat_axis=0, tiled=True
    )
    return jnp.sum(parts.astype(jnp.float32), axis=0)


MESH = pl.DeviceIdType.MESH
NT = (((1,), (1,)), ((), ()))
BF = jnp.bfloat16
F32 = jnp.float32


def flip(index, bits, top):
    total = 0
    while top:
        total = total + top * lax.rem(lax.rem(index // top, 2) + lax.rem(bits // top, 2), 2)
        top //= 2
    return total


def quarter_wave():
    half = math.pi / 2
    return [(-1.0) ** k * half ** (2 * k + 1) / math.factorial(2 * k + 1) for k in range(6)]


def turn_cos(index, period):
    quarter = period // 4
    x = (jnp.abs(index - 2 * quarter) - quarter).astype(F32) * (1.0 / quarter)
    y = x * x
    series = quarter_wave()
    value = series[-1]
    for term in series[-2::-1]:
        value = value * y + term
    return value * x


def fused_kernel(
    n_feed, n_time, n_frames, scale,
    volt, flags_in, window_in, slots_in, table_in, ua_in, pa_in, pb_in, out,
    vp, flags, window, slots, table, ua, pa, pb, result,
    coeffs, filt, spec, hist_out, hist_in, send_a, recv_a, send_b, recv_b,
    onehot, ns, acc, stacked,
    load_sem, in_sem, out_sem, own_sem, hist_sem, send_sem, recv_sem, bsend_sem, brecv_sem,
):
    me = lax.axis_index("feed")
    tm = lax.axis_index("tm")
    frame = 2 * CHANNELS
    past = TAPS - 1
    quads = n_frames // 4
    inputs = volt.shape[0]
    total = n_feed * inputs
    dests = n_feed * n_time
    rows_a = 4 * dests

    def load(f):
        return pltpu.make_async_copy(
            volt.at[:, pl.ds(f * frame, frame)], vp.at[f], load_sem.at[f]
        )

    tables = [
        (flags_in, flags), (window_in, window), (pa_in, pa), (slots_in, slots),
        (pb_in, pb), (ua_in, ua), (table_in, table),
    ]

    def fetch(k):
        return pltpu.make_async_copy(tables[k][0], tables[k][1], in_sem.at[k])

    fetch(0).start()
    fetch(1).start()
    for f in range(1, 8):
        load(f).start()
    barrier = pltpu.get_barrier_semaphore()

    def greet(i, _):
        pl.semaphore_signal(
            barrier, inc=1, device_id={"feed": flip(me, i // n_time, n_feed // 2), "tm": flip(tm, lax.rem(i, n_time), n_time // 2)},
            device_id_type=MESH,
        )
        return 0

    lax.fori_loop(1, dests, greet, 0)
    for f in list(range(8, n_frames)) + [0]:
        load(f).start()
    for k in range(2, len(tables)):
        fetch(k).start()

    def send_copy(q, i):
        m, t = i // n_time, lax.rem(i, n_time)
        to, tt = flip(me, m, n_feed // 2), flip(tm, t, n_time // 2)
        return pltpu.make_async_remote_copy(
            src_ref=send_a.at[q, to * n_time + tt],
            dst_ref=recv_a.at[pl.ds(pl.multiple_of((tm * quads + q) * 16, 16), 16), pl.ds(pl.multiple_of(me * inputs, 256), inputs)],
            send_sem=send_sem.at[q, i], recv_sem=recv_sem.at[q, i],
            device_id={"feed": to, "tm": tt}, device_id_type=MESH,
        )

    def arrival(q, i):
        m, t = i // n_time, lax.rem(i, n_time)
        to, tt = flip(me, m, n_feed // 2), flip(tm, t, n_time // 2)
        return pltpu.make_async_remote_copy(
            src_ref=send_a.at[q, to * n_time + tt],
            dst_ref=recv_a.at[pl.ds(pl.multiple_of((tt * quads + q) * 16, 16), 16), pl.ds(pl.multiple_of(to * inputs, 256), inputs)],
            send_sem=send_sem.at[q, i], recv_sem=recv_sem.at[q, i],
            device_id={"feed": to, "tm": tt}, device_id_type=MESH,
        )

    def own_copy(q):
        return pltpu.make_async_copy(
            send_a.at[q, me * n_time + tm],
            recv_a.at[pl.ds(pl.multiple_of((tm * quads + q) * 16, 16), 16), pl.ds(pl.multiple_of(me * inputs, 256), inputs)],
            own_sem.at[q],
        )

    def bsend_copy(i):
        m, t = i // n_time, lax.rem(i, n_time)
        to, tt = flip(me, m, n_feed // 2), flip(tm, t, n_time // 2)
        return pltpu.make_async_remote_copy(
            src_ref=send_b.at[to * n_time + tt],
            dst_ref=recv_b.at[pl.ds(pl.multiple_of(tm * 32, 32), 32), pl.ds(pl.multiple_of(me * inputs, 256), inputs)],
            send_sem=bsend_sem.at[i], recv_sem=brecv_sem.at[i],
            device_id={"feed": to, "tm": tt}, device_id_type=MESH,
        )

    def barrival(i):
        m, t = i // n_time, lax.rem(i, n_time)
        to, tt = flip(me, m, n_feed // 2), flip(tm, t, n_time // 2)
        return pltpu.make_async_remote_copy(
            src_ref=send_b.at[to * n_time + tt],
            dst_ref=recv_b.at[pl.ds(pl.multiple_of(tt * 32, 32), 32), pl.ds(pl.multiple_of(to * inputs, 256), inputs)],
            send_sem=bsend_sem.at[i], recv_sem=brecv_sem.at[i],
            device_id={"feed": to, "tm": tt}, device_id_type=MESH,
        )

    def bown_copy():
        return pltpu.make_async_copy(
            send_b.at[me * n_time + tm],
            recv_b.at[pl.ds(pl.multiple_of(tm * 32, 32), 32), pl.ds(pl.multiple_of(me * inputs, 256), inputs)],
            own_sem.at[quads],
        )

    def each(first, last, body):
        def step(i, _):
            body(i)
            return 0

        lax.fori_loop(first, last, step, 0)

    def hist_copy(to):
        return pltpu.make_async_remote_copy(
            src_ref=hist_out, dst_ref=hist_in, send_sem=hist_sem.at[0], recv_sem=hist_sem.at[1],
            device_id={"tm": to}, device_id_type=MESH,
        )

    fetch(0).wait()
    kept = flags[...].astype(F32)
    lane = lax.broadcasted_iota(jnp.int32, (128, 128), 1)
    sub = lax.broadcasted_iota(jnp.int32, (128, 128), 0)
    upto = jnp.dot(kept, jnp.where(sub <= lane, 1.0, 0.0), preferred_element_type=F32)
    whole = jnp.dot(kept, jnp.ones((128, 128), F32), preferred_element_type=F32)
    seen, before = [], jnp.zeros((1, 128), F32)
    for a in range(CHANNELS // 128):
        seen.append(upto[a : a + 1] + before)
        before = before + whole[a : a + 1]
    block = 48
    norm = 1.0 / math.sqrt(frame)

    def coeff_rows(r, _):
        row = lax.broadcasted_iota(jnp.int32, (block, 128), 0) + r * block
        step = lax.broadcasted_iota(jnp.int32, (block, 128), 1)
        early = row < rows_a
        dest = jnp.where(early, lax.shift_right_logical(row, 2), lax.shift_right_logical(row - rows_a, 1))
        chan = dest * LIVE_DEV + jnp.where(early, lax.shift_right_logical(row, 1) & 1, 2)
        chan = chan.astype(F32)
        shift = (row & 1) * (frame // 4)
        count = jnp.zeros((block, 128), F32)
        for one in seen:
            count = count + jnp.where(one <= chan, 1.0, 0.0)
        live = jnp.sum(count, axis=1, keepdims=True).astype(jnp.int32)
        fine = live * step
        fine_cos = turn_cos(fine & (frame - 1), frame)
        fine_sin = turn_cos((fine + 3 * frame // 4) & (frame - 1), frame)
        coarse = live * ((step & 15) * 128) + shift + jnp.where(step >= 16, 3 * frame // 4, 0)
        coarse = turn_cos(coarse & (frame - 1), frame) * norm
        at = pl.ds(pl.multiple_of(r * block, 16), block)
        for k in range(frame // 128):
            value = coarse[:, k : k + 1] * fine_cos - coarse[:, 16 + k : 17 + k] * fine_sin
            coeffs[at, k * 128 : (k + 1) * 128] = value.astype(BF)
        return 0

    lax.fori_loop(0, coeffs.shape[0] // block, coeff_rows, 0)
    fetch(1).wait()

    def filtered(f, slot, taps):
        for k in range(frame // 128):
            lanes = slice(k * 128, (k + 1) * 128)
            terms = {}
            for t in taps:
                w = jnp.concatenate([window[t, :, lanes]] * (inputs // 16), axis=0)
                terms[t] = w * vp[f + t - past, :, lanes]
            ends = [terms[t] for t in (0, past) if t in terms]
            middle = [terms[t] for t in range(1, past) if t in terms]
            parts = [functools.reduce(jnp.add, group) for group in (ends, middle) if group]
            filt[slot, :, lanes] = functools.reduce(jnp.add, parts)

    def spectra(slot):
        return lax.dot_general(coeffs[...], filt[slot], NT, preferred_element_type=F32)

    every = tuple(range(TAPS))

    def run(frames, keep):
        filtered(frames[0][0], 0, frames[0][1])
        for k in range(len(frames)):
            if k + 1 < len(frames):
                filtered(frames[k + 1][0], (k + 1) % 2, frames[k + 1][1])
            keep(k, spectra(k % 2))

    def pack(q):
        for j in range(rows_a // 32):
            data = jnp.concatenate([spec[4 * q + k, 32 * j : 32 * j + 32, :] for k in range(4)], axis=0)
            moved = jnp.dot(pa[...], data, preferred_element_type=F32)
            send_a[q, 8 * j : 8 * j + 8] = moved.astype(BF).reshape(8, 16, inputs)

    def send_quad(q):
        each(dests // 2, dests, lambda i: send_copy(q, i).start())
        each(1, dests // 2, lambda i: send_copy(q, i).start())
        own_copy(q).start()

    def middle_quad(q, _):
        for k in range(4):
            load(4 * q + k).wait()

        def keep(k, value):
            spec[4 * q + k] = value.astype(BF)

        run([(4 * q + k, every) for k in range(4)], keep)
        pack(q)

        @pl.when(q == 1)
        def _():
            pl.semaphore_wait(barrier, dests - 1)

        send_quad(q)
        return 0

    for f in range(1, 4):
        load(f).wait()
    fetch(2).wait()
    lax.fori_loop(1, quads, middle_quad, 0)

    def keep_tail(k, value):
        hist_out[k] = value.astype(BF)

    run([(n_frames + k, tuple(range(past - k))) for k in range(past)], keep_tail)

    @pl.when(tm < n_time - 1)
    def _():
        hist_copy(lax.rem(tm + 1, n_time)).start()

    fetch(3).wait()
    which = lax.broadcasted_iota(jnp.int32, (inputs, inputs), 0)

    def ones(g, _):
        for s in range(n_feed):
            hit = which == slots[s] - g * inputs
            onehot[pl.ds(pl.multiple_of(g * inputs, 256), inputs), s * inputs : (s + 1) * inputs] = jnp.where(hit, 1.0, 0.0).astype(BF)
        return 0

    load(0).wait()

    @pl.when(tm > 0)
    def _():
        hist_copy(lax.rem(tm + n_time - 1, n_time)).wait_recv()

    @pl.when(tm == 0)
    def _():
        hist_in[...] = jnp.zeros_like(hist_in)

    def keep_first(k, value):
        if k < past:
            value = value + hist_in[k].astype(F32)
        spec[k] = value.astype(BF)

    run([(k, tuple(range(max(past - k, 0), TAPS))) for k in range(4)], keep_first)
    pack(0)
    send_quad(0)
    fetch(4).wait()
    for j in range(dests // 8):
        data = jnp.concatenate([spec[f, rows_a + 16 * j : rows_a + 16 * j + 16, :] for f in range(n_frames)], axis=0)
        moved = jnp.dot(pb[...], data, preferred_element_type=F32)
        send_b[8 * j : 8 * j + 8] = moved.astype(BF).reshape(8, 32, inputs)
    each(dests // 2, dests, lambda i: bsend_copy(i).start())
    each(1, dests // 2, lambda i: bsend_copy(i).start())
    bown_copy().start()

    lax.fori_loop(0, n_feed, ones, 0)
    fetch(5).wait()
    fetch(6).wait()

    def wait_quad(q, _):
        own_copy(q).wait()
        each(1, dests, lambda i: arrival(q, i).wait_recv())
        return 0

    lax.fori_loop(0, quads, wait_quad, 0)
    half = 4 * n_time * UPCH // 4

    def beam_a(g, _):
        at = pl.ds(pl.multiple_of(g * inputs, 256), inputs)
        cells = lax.dot_general(recv_a[...], onehot[at, :], NT, preferred_element_type=F32).astype(BF)
        up = jnp.dot(ua[...], cells, preferred_element_type=F32).astype(BF)
        both = jnp.concatenate([
            jnp.concatenate([up[0:half], up[2 * half : 3 * half]], axis=0),
            jnp.concatenate([up[half : 2 * half], up[3 * half :]], axis=0),
        ], axis=1)
        value = jnp.dot(both, table[...], preferred_element_type=F32)
        ns[0, pl.ds(pl.multiple_of(g * half, half), half)] = value[:half]
        ns[1, pl.ds(pl.multiple_of(g * half, half), half)] = value[half:]
        return 0

    lax.fori_loop(0, n_feed, beam_a, 0)

    def power(c, chan):
        for e0 in range(NS // 128):
            lanes = slice(e0 * 128, e0 * 128 + 128)
            more = slice(NS + e0 * 128, NS + e0 * 128 + 128)
            sums = [0.0] * CYL
            for p in range(2):
                z = []
                for y in range(CYL):
                    at = slice((p * CYL + y) * half, (p * CYL + y + 1) * half)
                    z.append((ns[c, at, lanes], ns[c, at, more]))
                (r0, i0), (r1, i1), (r2, i2), (r3, i3) = z
                t0r, t1r, t2r, t3r = r0 + r2, r0 - r2, r1 + r3, r1 - r3
                t0i, t1i, t2i, t3i = i0 + i2, i0 - i2, i1 + i3, i1 - i3
                re = [t0r + t2r, t1r + t3i, t0r - t2r, t1r - t3i]
                im = [t0i + t2i, t1i - t3r, t0i - t2i, t1i + t3r]
                for e in range(CYL):
                    sums[e] = sums[e] + re[e] * re[e] + im[e] * im[e]
            for e in range(CYL):
                parts = sums[e].reshape(n_time, UPCH, 128)
                value = parts[0]
                for t in range(1, n_time):
                    value = value + parts[t]
                result[chan, :, e * NS + e0 * 128 : e * NS + e0 * 128 + 128] = value * scale

    def out_copy(c):
        return pltpu.make_async_copy(result.at[c], out.at[c], out_sem.at[c])

    power(0, 0)
    power(1, 1)
    out_copy(0).start()
    out_copy(1).start()

    bown_copy().wait()
    each(1, dests // 2, lambda i: barrival(i).wait_recv())
    home = pl.multiple_of(me // (n_feed // 2) * (total // 2), 256)

    def near(g, _):
        at = pl.ds(pl.multiple_of(g * inputs, 256), inputs)
        near_cols = pl.ds(home, total // 2)
        acc[g] = lax.dot_general(recv_b[:, near_cols], onehot[at, near_cols], NT, preferred_element_type=F32)
        return 0

    lax.fori_loop(0, n_feed, near, 0)

    def source(m, _):
        each(m * n_time, (m + 1) * n_time, lambda i: barrival(i).wait_recv())
        cols = pl.ds(pl.multiple_of(flip(me, m, n_feed // 2) * inputs, 256), inputs)

        def add(g, _):
            at = pl.ds(pl.multiple_of(g * inputs, 256), inputs)
            acc[g] += lax.dot_general(recv_b[:, cols], onehot[at, cols], NT, preferred_element_type=F32)
            return 0

        lax.fori_loop(0, n_feed, add, 0)
        return 0

    lax.fori_loop(n_feed // 2, n_feed - 1, source, 0)
    last = n_feed - 1
    each(last * n_time, (last + 1) * n_time, lambda i: barrival(i).wait_recv())
    cols = pl.ds(pl.multiple_of(flip(me, last, n_feed // 2) * inputs, 256), inputs)
    for g in range(n_feed):
        got = lax.dot_general(recv_b[:, cols], onehot[g * inputs : (g + 1) * inputs, cols], NT, preferred_element_type=F32)
        got = (acc[g] + got).astype(BF).reshape(n_time, 2, UPCH, inputs)
        for part in range(2):
            stacked[g * half : (g + 1) * half, part * inputs : (part + 1) * inputs] = got[:, part].reshape(half, inputs)
    ns[0] = jnp.dot(stacked[...], table[...], preferred_element_type=F32)
    power(0, 2)
    out_copy(2).start()

    def drain(q, _):
        each(1, dests, lambda i: send_copy(q, i).wait_send())
        return 0

    lax.fori_loop(0, quads, drain, 0)
    each(1, dests, lambda i: bsend_copy(i).wait_send())

    @pl.when(tm < n_time - 1)
    def _():
        hist_copy(lax.rem(tm + 1, n_time)).wait_send()

    for c in range(LIVE_DEV):
        out_copy(c).wait()


def rounded_pair(modulus, first, second):
    angle = (first[:, None] * second[None, :] % modulus) * (2.0 * np.pi / modulus)
    scale = 1.0 / np.sqrt(modulus)
    return (
        (np.cos(angle) * scale).astype(np.float32).astype(BF),
        (np.sin(angle) * scale).astype(np.float32).astype(BF),
    )


def window_table():
    length = TAPS * 2 * CHANNELS
    sample = np.arange(length)
    offset = (sample - length / 2 + 0.5) / (2 * CHANNELS)
    taper = 0.5 - 0.5 * np.cos(2.0 * np.pi * (sample + 0.5) / length)
    return (np.sinc(offset) * taper).astype(np.float32).reshape(TAPS, 2 * CHANNELS)


def up_matrix(frames):
    c, s = rounded_pair(UPCH, np.arange(UPCH), np.arange(frames))
    c, s = c.astype(np.float32), s.astype(np.float32)
    return np.stack([np.stack([c, s], -1), np.stack([-s, c], -1)])


def row_tables(n_frames, n_time):
    up = up_matrix(n_frames)
    pa = np.einsum("da,fb,xc->dfxbac", np.eye(8), np.eye(4), np.eye(4)).reshape(128, 128)
    pb = np.einsum("da,vkfr->dvkfar", np.eye(8), up).reshape(8 * 2 * UPCH, n_frames * 16)
    ua = np.einsum("gc,tb,vkfr->gvtkbfcr", np.eye(2), np.eye(n_time), up)
    ua = ua.reshape(4 * n_time * UPCH, n_time * n_frames * 4)
    return [jnp.array(one.astype(np.float32).astype(BF)) for one in (ua, pa, pb)]


def local_fused(voltages, feed_slot, channel_flags):
    frame = 2 * CHANNELS
    inputs = voltages.shape[0]
    n_frames = voltages.shape[1] // frame
    n_time = lax.axis_size("tm")
    n_feed = lax.axis_size("feed")
    quads = n_frames // 4
    dests = n_feed * n_time
    rows = 2 * LIVE_DEV * dests
    total = n_feed * inputs
    index = np.arange(NS)
    c, d = rounded_pair(NS, index, index)
    table = jnp.array(np.concatenate([np.concatenate([c, -d], axis=1), np.concatenate([d, c], axis=1)], axis=0))
    ua, pa, pb = row_tables(n_frames, n_time)
    window = jnp.array(np.repeat(window_table().astype(BF)[:, None, :], 16, axis=1))
    operands = [
        voltages, channel_flags.reshape(CHANNELS // 128, 128), window, feed_slot.reshape(n_feed, 1, inputs),
        table, ua, pa, pb,
    ]
    dma = pltpu.SemaphoreType.DMA
    staged = [pltpu.VMEM(one.shape, one.dtype) for one in operands[1:]]
    half = n_time * UPCH
    return pl.pallas_call(
        functools.partial(fused_kernel, n_feed, n_time, n_frames, 0.25 / (2.0 * n_time)),
        out_shape=jax.ShapeDtypeStruct((LIVE_DEV, UPCH, CYL * NS), F32),
        in_specs=[pl.BlockSpec(memory_space=pl.ANY)] * len(operands),
        out_specs=pl.BlockSpec(memory_space=pl.ANY),
        scratch_shapes=[pltpu.VMEM((n_frames, inputs, frame), BF)] + staged + [
            pltpu.VMEM((LIVE_DEV, UPCH, CYL * NS), F32),
            pltpu.VMEM((rows, frame), BF),
            pltpu.VMEM((2, inputs, frame), BF),
            pltpu.VMEM((n_frames, rows, inputs), BF),
            pltpu.VMEM((TAPS - 1, rows, inputs), BF),
            pltpu.VMEM((TAPS - 1, rows, inputs), BF),
            pltpu.VMEM((quads, dests, 16, inputs), BF),
            pltpu.VMEM((n_time * quads * 16, total), BF),
            pltpu.VMEM((dests, 2 * UPCH, inputs), BF),
            pltpu.VMEM((n_time * 2 * UPCH, total), BF),
            pltpu.VMEM((total, total), BF),
            pltpu.VMEM((2, n_feed * half, 2 * NS), F32),
            pltpu.VMEM((n_feed, 2 * half, NS), F32),
            pltpu.VMEM((n_feed * half, 2 * NS), BF),
            dma((n_frames,)),
            dma((len(operands) - 1,)),
            dma((LIVE_DEV,)),
            dma((quads + 1,)),
            dma((2,)),
            dma((quads, dests)),
            dma((quads, dests)),
            dma((dests,)),
            dma((dests,)),
        ],
        compiler_params=pltpu.CompilerParams(
            collective_id=0, has_side_effects=True, vmem_limit_bytes=62 * 1024 * 1024
        ),
    )(*operands)


def local(voltages, feed_slot, channel_flags):
    fits = (
        voltages.shape[0] == NS
        and voltages.shape[1] == UPCH * 2 * CHANNELS
        and lax.axis_size("tm") == 4
        and lax.axis_size("feed") == 8
        and lax.axis_size("feed") * voltages.shape[0] == 2 * CYL * NS
    )
    return (local_fused if fits else local_plain)(voltages, feed_slot, channel_flags)


def solution(mesh):
    in_specs = (P("feed", "tm"), P(), P())
    out_specs = P(("feed", "tm"), None, None)
    return jax.shard_map(local, mesh=mesh, in_specs=in_specs, out_specs=out_specs, check_vma=False)
```

time: 68.6 us -> 65.6 us (0.956)
  the two profiles are of different devices: /device:TPU:0 before, /device:TPU:9 now
where the time goes in v1:
time: 65.6 us; the launch traced here: 65.5 us
  Pallas kernels  63.8 us (97%)
  local copies, waits for them, and re-layouts  1.62 us (2%)
    pallas_call x1, Pallas kernels, local_fused(): pl.pallas_call(functools.partial(fused_kernel, n_feed, n_time, n_frames,...  63.8 us
    unnamed x1, local copies, waits for them, and re-layouts  1.62 us

profile of v1, /device:TPU:9, one launch (start us, length us, event | category | flops | bytes accessed | tf_op | source)
XLA Modules:
  0.0 65.5 jit_solution(2450730389638291143)
XLA Ops:
  0.0 63.8 %shard_map.82 = f32[3,16,1024]{2,1,0:T(8,128)} custom-call(bf16[256,32768]{1,0:T(8,128)(2,1)} %volt.1, s32[8,128]{1,0:T(8,128)} %bitcast.3, bf16[4,16,2048]{2,1,0:T(8,128)(2,1)} %constant.14.clone.window_in, s32[8,1,256]{2,1,0:T(1,128)} %bitcast.2, bf16[512,512]{1,0:T(8,128)(2,1)} %constant.10.clone.table_in, bf16[256,256]{1,0:T(8,128)(2,1)} %constant.11.clone.ua_in, ...), custom_call_target="tpu_custom_call" | custom-call | tf_op jit(solution)/shard_map/pallas_call | solution.py:575
  63.8 1.6 %copy.10 = f32[3,16,1024]{2,1,0:T(8,128)} copy(f32[3,16,1024]{2,1,0:T(8,128)} %shard_map.82) | data formatting | bytes 393216
